TPU v7x, 256 devices: a whole 4x4x8 slice. The times are simulated.
256 devices in a mesh: rows: 32 (over x, z_hi, core), cols: 8 (over z_lo, y).
Axes of the slice: x: 4, y: 4, z: 8 (z_hi: 4, z_lo: 2; z = z_hi * 2 + z_lo), core: 2. Of those that a mesh axis runs over, the one named last changes fastest.
Arguments:
- right_side: float32 [4, 8, 1024, 512], P(None, 'cols', 'rows'), may hold values from -6 to 6
- inverse_blocks: bfloat16 [4, 8, 1024, 8192], P(None, None, 'rows', 'cols'), may hold values from -0.09375 to 0.09375
- lower_blocks: bfloat16 [6, 8, 1024, 8192], P(None, None, 'rows', 'cols'), may hold values from -0.046875 to 0.046875
Outputs:
- solution: float32 [4, 8, 1024, 512], P(None, 'cols', 'rows')
All inputs are finite; a program needn't handle non-finite values.
Results may differ from a plain program's by a relative error of at most 0.014.
Values may be sent and summed in bfloat16 or wider, within the bound.
A program may use at most 64 MiB of HBM per device.

v0:
```python
import jax
import jax.numpy as jnp
from jax import lax
from jax.sharding import PartitionSpec as P


def pair_index(target, source):
    return target * (target - 1) // 2 + source


def product(factor_block, rows_all):
    return jnp.einsum("abk,kn->abn", factor_block, rows_all, preferred_element_type=jnp.float32)


def fold_rows(factor_block, incoming):
    return jnp.einsum("abk,kn->abn", factor_block, incoming[0], preferred_element_type=jnp.float32)


def forward_solve(right_side, inverse_blocks, lower_blocks):
    panels = right_side.shape[0]
    groups = inverse_blocks.shape[1]
    local_rows = inverse_blocks.shape[2]
    columns = right_side.shape[3]
    gathered = []
    solutions = []
    for current in range(panels):
        if current == 0:
            residual = right_side[0].astype(jnp.bfloat16)
        else:
            partial_value = jnp.zeros((groups, local_rows, columns), jnp.float32)
            for source in range(current):
                partial_value = partial_value + product(
                    lower_blocks[pair_index(current, source)], gathered[source]
                )
            shares = lax.psum_scatter(partial_value, "cols", scatter_dimension=0, tiled=True)
            residual = (right_side[current] - shares).astype(jnp.bfloat16)
        products = fold_rows(
            inverse_blocks[current], lax.all_gather(residual, "rows", axis=1, tiled=True)
        )
        solved = lax.psum_scatter(products, "cols", scatter_dimension=0, tiled=True)
        solutions.append(solved)
        if current + 1 < panels:
            rows_all = lax.all_gather(solved.astype(jnp.bfloat16), "rows", axis=1, tiled=True)[0]
            gathered.append(rows_all)
    return jnp.stack(solutions)


def body(right_side, inverse_blocks, lower_blocks):
    return forward_solve(right_side, inverse_blocks, lower_blocks)


def solution(mesh):
    return jax.shard_map(
        body,
        mesh=mesh,
        in_specs=(
            P(None, "cols", "rows", None),
            P(None, None, "rows", "cols"),
            P(None, None, "rows", "cols"),
        ),
        out_specs=P(None, "cols", "rows", None),
        check_vma=False,
    )
```

profile of v0, /device:TPU:1, one launch (start us, length us, event | category | flops | bytes accessed | tf_op | source)
XLA Modules:
  0.0 673.5 jit_solution(5792396489258277267)
XLA Ops:
  6.5 1.5 slice.102
  8.1 58.1 %all-gather.21.cloned.1.call-done = bf16[1,1,1024,512]{3,2,1,0:T(8,128)(2,1)} async-done(((bf16[1,1,32,512]{3,2,1,0:T(8,128)(2,1)}), bf16[1,1,1024,512]{3,2,1,0:T(8,128)(2,1)}) %all-gather.21.cloned.1.call-update) | async-done | bytes 1048592 | tf_op jit(solution)/shard_map/all_gather | solution.py:38
  66.2 2.6 fusion.2
  68.9 32.4 %reduce-scatter.8.cloned.1.call-done = f32[1,32,512]{2,1,0:T(8,128)} async-done(((f32[8,32,512]{2,1,0:T(8,128)}), f32[1,32,512]{2,1,0:T(8,128)}) %reduce-scatter.8.cloned.1.call-update) | async-done | bytes 65552 | tf_op jit(solution)/shard_map/reduce_scatter | solution.py:40
  101.4 1.5 convert_element_type.31
  102.9 57.6 %all-gather.9.cloned.1.call-done = bf16[1,1024,512]{2,1,0:T(8,128)(2,1)} async-done(((bf16[1,32,512]{2,1,0:T(8,128)(2,1)}), bf16[1,1024,512]{2,1,0:T(8,128)(2,1)}) %all-gather.9.cloned.1.call-update) | async-done | bytes 1048592 | tf_op jit(solution)/shard_map/all_gather | solution.py:43
  160.5 2.6 convolution_bitcast_fusion.3
  163.2 32.5 %reduce-scatter.10.cloned.1.call-done = f32[1,32,512]{2,1,0:T(8,128)} async-done(((f32[8,32,512]{2,1,0:T(8,128)}), f32[1,32,512]{2,1,0:T(8,128)}) %reduce-scatter.10.cloned.1.call-update) | async-done | bytes 65552 | tf_op jit(solution)/shard_map/reduce_scatter | solution.py:35
  195.7 1.5 fusion.37
  197.2 57.1 %all-gather.11.cloned.1.call-done = bf16[1,1024,512]{2,1,0:T(8,128)(2,1)} async-done(((bf16[1,32,512]{2,1,0:T(8,128)(2,1)}), bf16[1,1024,512]{2,1,0:T(8,128)(2,1)}) %all-gather.11.cloned.1.call-update) | async-done | bytes 1048592 | tf_op jit(solution)/shard_map/all_gather | solution.py:38
  254.3 2.5 convolution_bitcast_fusion.2
  256.9 32.4 %reduce-scatter.12.cloned.1.call-done = f32[1,32,512]{2,1,0:T(8,128)} async-done(((f32[8,32,512]{2,1,0:T(8,128)}), f32[1,32,512]{2,1,0:T(8,128)}) %reduce-scatter.12.cloned.1.call-update) | async-done | bytes 65552 | tf_op jit(solution)/shard_map/reduce_scatter | solution.py:40
  289.3 1.5 convert_element_type.33
  290.8 1.8 fusion.12
  292.6 55.8 %all-gather.13.cloned.1.call-done = bf16[1,1024,512]{2,1,0:T(8,128)(2,1)} async-done(((bf16[1,32,512]{2,1,0:T(8,128)(2,1)}), bf16[1,1024,512]{2,1,0:T(8,128)(2,1)}) %all-gather.13.cloned.1.call-update) | async-done | bytes 1048592 | tf_op jit(solution)/shard_map/all_gather | solution.py:43
  348.4 2.6 fusion.1
  351.1 32.4 %reduce-scatter.14.cloned.1.call-done = f32[1,32,512]{2,1,0:T(8,128)} async-done(((f32[8,32,512]{2,1,0:T(8,128)}), f32[1,32,512]{2,1,0:T(8,128)}) %reduce-scatter.14.cloned.1.call-update) | async-done | bytes 65552 | tf_op jit(solution)/shard_map/reduce_scatter | solution.py:35
  383.5 1.5 fusion.36
  385.1 57.3 %all-gather.15.cloned.1.call-done = bf16[1,1024,512]{2,1,0:T(8,128)(2,1)} async-done(((bf16[1,32,512]{2,1,0:T(8,128)(2,1)}), bf16[1,1024,512]{2,1,0:T(8,128)(2,1)}) %all-gather.15.cloned.1.call-update) | async-done | bytes 1048592 | tf_op jit(solution)/shard_map/all_gather | solution.py:38
  442.4 2.5 convolution_bitcast_fusion.1
  444.9 32.5 %reduce-scatter.16.cloned.1.call-done = f32[1,32,512]{2,1,0:T(8,128)} async-done(((f32[8,32,512]{2,1,0:T(8,128)}), f32[1,32,512]{2,1,0:T(8,128)}) %reduce-scatter.16.cloned.1.call-update) | async-done | bytes 65552 | tf_op jit(solution)/shard_map/reduce_scatter | solution.py:40
  477.4 1.5 convert_element_type.35
  478.9 1.8 fusion.10
  480.7 1.8 convolution_add_fusion.1
  482.5 54.0 %all-gather.17.cloned.1.call-done = bf16[1,1024,512]{2,1,0:T(8,128)(2,1)} async-done(((bf16[1,32,512]{2,1,0:T(8,128)(2,1)}), bf16[1,1024,512]{2,1,0:T(8,128)(2,1)}) %all-gather.17.cloned.1.call-update) | async-done | bytes 1048592 | tf_op jit(solution)/shard_map/all_gather | solution.py:43
  536.5 2.6 fusion
  539.1 32.4 %reduce-scatter.18.cloned.1.call-done = f32[1,32,512]{2,1,0:T(8,128)} async-done(((f32[8,32,512]{2,1,0:T(8,128)}), f32[1,32,512]{2,1,0:T(8,128)}) %reduce-scatter.18.cloned.1.call-update) | async-done | bytes 65552 | tf_op jit(solution)/shard_map/reduce_scatter | solution.py:35
  571.5 1.5 fusion.35
  573.1 57.3 %all-gather.19.cloned.1.call-done = bf16[1,1024,512]{2,1,0:T(8,128)(2,1)} async-done(((bf16[1,32,512]{2,1,0:T(8,128)(2,1)}), bf16[1,1024,512]{2,1,0:T(8,128)(2,1)}) %all-gather.19.cloned.1.call-update) | async-done | bytes 1048592 | tf_op jit(solution)/shard_map/all_gather | solution.py:38
  630.4 2.5 convolution_bitcast_fusion
  632.9 32.5 %reduce-scatter.20.cloned.1.call-done = f32[1,32,512]{2,1,0:T(8,128)} async-done(((f32[8,32,512]{2,1,0:T(8,128)}), f32[1,32,512]{2,1,0:T(8,128)}) %reduce-scatter.20.cloned.1.call-update) | async-done | bytes 65552 | tf_op jit(solution)/shard_map/reduce_scatter | solution.py:40
  665.4 1.6 pad_maximum_fusion
  (38 shorter events, 0.8 us)
Async XLA Ops:
  6.5 59.7 %all-gather.21.cloned.1.call-start = ((), (), s32[]{:S(2)}) async-start(), calls=%async_computation.20 | async-start | bytes 1081344 | tf_op jit(solution)/shard_map/all_gather | solution.py:38
  8.0 187.6 %copy-start.3 = (f32[4,1,32,512]{3,2,1,0:T(8,128)S(1)}, f32[4,1,32,512]{3,2,1,0:T(8,128)}, u32[]{:S(2)}) copy-start(f32[4,1,32,512]{3,2,1,0:T(8,128)} %param.3) | copy-start | bytes 786436
  8.0 93.3 %reduce-scatter.8.cloned.1.call-start = ((), (), s32[]{:S(2)}) async-start(), calls=%async_computation.7 | async-start | bytes 589824 | tf_op jit(solution)/shard_map/reduce_scatter | solution.py:40
  68.8 185.5 %copy-start.4 = (bf16[4,8,32,1024]{3,2,1,0:T(8,128)(2,1)S(1)}, bf16[4,8,32,1024]{3,2,1,0:T(8,128)(2,1)}, u32[]{:S(2)}) copy-start(bf16[4,8,32,1024]{3,2,1,0:T(8,128)(2,1)} %param.4) | copy-start | bytes 6291460
  68.9 91.6 %all-gather.9.cloned.1.call-start = ((), (), s32[]{:S(2)}) async-start(), calls=%async_computation.8 | async-start | bytes 1081344 | tf_op jit(solution)/shard_map/all_gather | solution.py:43
  102.8 92.8 %reduce-scatter.10.cloned.1.call-start = ((), (), s32[]{:S(2)}) async-start(), calls=%async_computation.9 | async-start | bytes 589824 | tf_op jit(solution)/shard_map/reduce_scatter | solution.py:35
  163.1 91.2 %all-gather.11.cloned.1.call-start = ((), (), s32[]{:S(2)}) async-start(), calls=%async_computation.10 | async-start | bytes 1081344 | tf_op jit(solution)/shard_map/all_gather | solution.py:38
  197.2 92.1 %reduce-scatter.12.cloned.1.call-start = ((), (), s32[]{:S(2)}) async-start(), calls=%async_computation.11 | async-start | bytes 589824 | tf_op jit(solution)/shard_map/reduce_scatter | solution.py:40
  256.8 91.6 %all-gather.13.cloned.1.call-start = ((), (), s32[]{:S(2)}) async-start(), calls=%async_computation.12 | async-start | bytes 1081344 | tf_op jit(solution)/shard_map/all_gather | solution.py:43
  290.8 92.7 %reduce-scatter.14.cloned.1.call-start = ((), (), s32[]{:S(2)}) async-start(), calls=%async_computation.13 | async-start | bytes 589824 | tf_op jit(solution)/shard_map/reduce_scatter | solution.py:35
  351.0 91.3 %all-gather.15.cloned.1.call-start = ((), (), s32[]{:S(2)}) async-start(), calls=%async_computation.14 | async-start | bytes 1081344 | tf_op jit(solution)/shard_map/all_gather | solution.py:38
  385.0 92.4 %reduce-scatter.16.cloned.1.call-start = ((), (), s32[]{:S(2)}) async-start(), calls=%async_computation.15 | async-start | bytes 589824 | tf_op jit(solution)/shard_map/reduce_scatter | solution.py:40
  444.8 91.6 %all-gather.17.cloned.1.call-start = ((), (), s32[]{:S(2)}) async-start(), calls=%async_computation.16 | async-start | bytes 1081344 | tf_op jit(solution)/shard_map/all_gather | solution.py:43
  478.8 92.7 %reduce-scatter.18.cloned.1.call-start = ((), (), s32[]{:S(2)}) async-start(), calls=%async_computation.17 | async-start | bytes 589824 | tf_op jit(solution)/shard_map/reduce_scatter | solution.py:35
  539.1 126.3 %copy-start = (f32[1,32,512]{2,1,0:T(8,128)S(1)}, f32[1,32,512]{2,1,0:T(8,128)}, u32[]{:S(2)}) copy-start(f32[1,32,512]{2,1,0:T(8,128)} %reduce-scatter.8.cloned.1.call-done) | copy-start | bytes 196612
  539.1 126.3 %copy-start.1 = (f32[1,32,512]{2,1,0:T(8,128)S(1)}, f32[1,32,512]{2,1,0:T(8,128)}, u32[]{:S(2)}) copy-start(f32[1,32,512]{2,1,0:T(8,128)} %reduce-scatter.12.cloned.1.call-done) | copy-start | bytes 196612
  539.1 126.3 %copy-start.2 = (f32[1,32,512]{2,1,0:T(8,128)S(1)}, f32[1,32,512]{2,1,0:T(8,128)}, u32[]{:S(2)}) copy-start(f32[1,32,512]{2,1,0:T(8,128)} %reduce-scatter.16.cloned.1.call-done) | copy-start | bytes 196612
  539.1 91.3 %all-gather.19.cloned.1.call-start = ((), (), s32[]{:S(2)}) async-start(), calls=%async_computation.18 | async-start | bytes 1081344 | tf_op jit(solution)/shard_map/all_gather | solution.py:38
  573.0 92.4 %reduce-scatter.20.cloned.1.call-start = ((), (), s32[]{:S(2)}) async-start(), calls=%async_computation.19 | async-start | bytes 589824 | tf_op jit(solution)/shard_map/reduce_scatter | solution.py:40
Sparse Core Ops, SparseCore 0:
  9.9 56.2 all-gather.20
  69.0 32.3 reduce-scatter.7
  104.2 56.2 all-gather.8
  163.3 32.3 reduce-scatter.9
  198.1 56.2 all-gather.10
  256.9 32.3 reduce-scatter.11
  292.2 56.2 all-gather.12
  351.2 32.3 reduce-scatter.13
  386.1 56.2 all-gather.14
  445.0 32.3 reduce-scatter.15
  480.2 56.1 all-gather.16
  539.2 32.2 reduce-scatter.17
  574.1 56.2 all-gather.18
  633.0 32.3 reduce-scatter.19
where the time goes:
time: 678 us; the launch traced here: 673 us
  waiting for transfers between devices  625 us (92%)
  matrix products  23.2 us (3%)
  between operations  13.3 us (2%)
  other arithmetic  10.3 us (2%)
    all_gather x4, waiting for transfers between devices, forward_solve(): lax.all_gather(residual, 'rows', axis=1, tiled=True)  230 us
    all_gather x3, waiting for transfers between devices, forward_solve(): lax.all_gather(solved.astype(jnp.bfloat16), 'rows', axis=1, tiled=True)[0]  167 us
    reduce_scatter x4, waiting for transfers between devices, forward_solve(): solved = lax.psum_scatter(products, 'cols', scatter_dimension=0, tiled=True)  130 us
    reduce_scatter x3, waiting for transfers between devices, forward_solve(): lax.psum_scatter(partial_value, 'cols', scatter_dimension=0, tiled=True)  97.3 us
  transfers between devices with their start and end apart: 14, of which 14 were waited for; matrix products, arithmetic and copies ran while one was open for 1% of the time, Pallas kernels for 0%

commit v1 on v0

v1 whole, which is shorter than its diff:
```python
import functools

import jax
import jax.numpy as jnp
from jax import lax
from jax.experimental import pallas as pl
from jax.experimental.pallas import tpu as pltpu
from jax.sharding import PartitionSpec as P

MESH = pl.DeviceIdType.MESH
X, ZH, CORE, ZL, Y = 4, 4, 2, 2, 4
LANES = 128
BF16, F32 = jnp.bfloat16, jnp.float32


def pair_index(target, source):
    return target * (target - 1) // 2 + source


def device(x, zh, core, zl, y):
    return {"rows": (x * ZH + zh) * CORE + core, "cols": zl * Y + y}


def solve_kernel(
    panels, rhs, inv, low, out, fac, bb, g, part, recv, xo, acc, early,
    b_loc, b_send, b_recv, f_loc, f_send, f_recv, rs_send, rs_recv,
    z_send, z_recv, x_send, x_recv, o_loc, o_send, o_recv,
):
    groups = inv.shape[1]
    rows = inv.shape[2]
    block = rows * CORE
    half = rhs.shape[3] // CORE
    chunks = half // LANES
    wide = ZH * block
    height = groups * block

    r = lax.axis_index("rows")
    c = lax.axis_index("cols")
    x, zh, core = r // (ZH * CORE), (r // CORE) % ZH, r % CORE
    zl, y = c // Y, c % Y
    other = 1 - core

    mate = device(x, zh, other, zl, y)
    col_peers = {
        (dz, dy): device(x, zh, core, (zl + dz) % ZL, (y + dy) % Y)
        for dz in range(ZL) for dy in range(Y) if (dz, dy) != (0, 0)
    }
    z_peers = {d: device(x, (zh + d) % ZH, core, zl, y) for d in range(1, ZH)}
    x_peers = {d: device((x + d) % X, zh, core, zl, y) for d in range(1, X)}
    far_cols = sorted(col_peers, key=lambda o: -(o[0] + min(o[1], Y - o[1])))
    far_z = sorted(z_peers, key=lambda d: -min(d, ZH - d))
    far_x = sorted(x_peers, key=lambda d: -min(d, X - d))

    def remote(src, dst, send, recv_sem, peer):
        return pltpu.make_async_remote_copy(
            src_ref=src, dst_ref=dst, send_sem=send, recv_sem=recv_sem,
            device_id=peer, device_id_type=MESH,
        )

    def take(ref, sem):
        pltpu.make_async_copy(ref, ref, sem).wait()

    mine = pl.ds(pl.multiple_of(core * rows, rows), rows)
    theirs = pl.ds(pl.multiple_of(other * rows, rows), rows)
    my_half = pl.ds(pl.multiple_of(core * half, half), half)
    their_half = pl.ds(pl.multiple_of(other * half, half), half)

    def factor_source(f):
        return inv.at[f] if f < panels else low.at[f - panels]

    def rhs_local(p):
        return pltpu.make_async_copy(
            rhs.at[p, 0, :, my_half], bb.at[p, mine, :], b_loc.at[p])

    def rhs_remote(p):
        return remote(
            rhs.at[p, 0, :, their_half], bb.at[p, mine, :],
            b_send.at[p], b_recv.at[p], mate)

    def factor_local(f):
        return pltpu.make_async_copy(factor_source(f), fac.at[f, :, mine, :], f_loc.at[f])

    def factor_remote(f):
        return remote(
            factor_source(f), fac.at[f, :, mine, :], f_send.at[f], f_recv.at[f], mate)

    stages = []
    order = []
    for p in range(panels):
        if p > 0:
            stages.append((p, False))
            order += [panels + pair_index(p, q) for q in reversed(range(p))]
        stages.append((p, True))
        order.append(p)

    rhs_local(0).start()
    factor_local(0).start()
    barrier = pltpu.get_barrier_semaphore()
    everyone = [mate, *col_peers.values(), *z_peers.values(), *x_peers.values()]
    for peer in everyone:
        pl.semaphore_signal(barrier, inc=1, device_id=peer, device_id_type=MESH)
    pl.semaphore_wait(barrier, len(everyone))
    rhs_remote(0).start()
    factor_remote(0).start()

    home = (x * ZH + zh) * block
    here = pl.ds(pl.multiple_of(home, block), block)

    def gather_start(s, h):
        own = g.at[s, h, here, :]
        for d in far_z:
            remote(own, own, z_send.at[s, h], z_recv.at[s, h, d - 1], z_peers[d]).start()
        for d in far_x:
            remote(own, own, x_send.at[s, h], x_recv.at[s, h, d - 1], x_peers[d]).start()

    def gather_relay(s, h):
        for d in far_z[::-1]:
            source = (zh - d) % ZH
            place = pl.ds(pl.multiple_of((x * ZH + source) * block, block), block)
            piece = g.at[s, h, place, :]
            take(piece, z_recv.at[s, h, d - 1])
            for e in far_x:
                remote(piece, piece, x_send.at[s, h], x_recv.at[s, h, e - 1], x_peers[e]).start()

    def plane(d):
        return pl.ds(pl.multiple_of(((x - d) % X) * wide, wide), wide)

    def product(f, s, h, span):
        factor = fac[f, :, :, span].reshape(height, -1)
        return jnp.dot(factor, g[s, h, span, :], preferred_element_type=F32)

    everything = pl.ds(0, X * wide)
    loaded = set()

    def need(f):
        if f not in loaded:
            loaded.add(f)
            factor_local(f).wait()
            take(fac.at[f, :, mine, :], f_recv.at[f])

    def main_factor(s):
        p, inverse = stages[s]
        return p if inverse else panels + pair_index(p, p - 1)

    def relay_and_first(s, h):
        p, inverse = stages[s]
        gather_relay(s, h)
        f = main_factor(s)
        need(f)
        first = product(f, s, h, plane(0))
        if not inverse and p >= 2:
            first = first + early[p - 2, h]
        acc[h] = first

    def finish_product(s, h):
        p, inverse = stages[s]
        f = main_factor(s)
        for d in far_x[::-1]:
            take(g.at[s, h, plane(d), :], x_recv.at[s, h, d - 1])
            acc[h] = acc[h] + product(f, s, h, plane(d))
        part[s, h] = acc[h].astype(BF16)
        for dz, dy in far_cols:
            group = ((zl + dz) % ZL) * Y + (y + dy) % Y
            rows_there = pl.ds(pl.multiple_of(group * block, block), block)
            remote(
                part.at[s, h, rows_there, :], recv.at[s, h, dz * Y + dy],
                rs_send.at[s, h], rs_recv.at[s, h], col_peers[dz, dy],
            ).start()
        if not inverse:
            for later in range(p + 1, panels):
                extra_factor = panels + pair_index(later, p - 1)
                need(extra_factor)
                extra = product(extra_factor, s, h, everything)
                if p > 1:
                    extra = extra + early[later - 2, h]
                early[later - 2, h] = extra

    def out_local(p, h):
        there = pl.ds(pl.multiple_of(core * half + h * LANES, LANES), LANES)
        return pltpu.make_async_copy(
            xo.at[p, h, mine, :], out.at[p, 0, :, there], o_loc.at[p, h])

    def out_remote(p, h):
        there = pl.ds(pl.multiple_of(core * half + h * LANES, LANES), LANES)
        return remote(
            xo.at[p, h, theirs, :], out.at[p, 0, :, there],
            o_send.at[p, h], o_recv.at[p, h], mate)

    def reduce_and_send(s, h):
        p, inverse = stages[s]
        take(recv.at[s, h, pl.ds(1, groups - 1)], rs_recv.at[s, h])
        total = acc[h, pl.ds(pl.multiple_of(c * block, block), block), :]
        for slot in range(1, groups):
            total = total + recv[s, h, slot].astype(F32)
        if inverse:
            xo[p, h] = total
            value = total
        else:
            value = bb[p, :, pl.ds(h * LANES, LANES)] - total
        if s + 1 < len(stages):
            g[s + 1, h, here, :] = value.astype(BF16)
            gather_start(s + 1, h)
        if inverse:
            out_local(p, h).start()
            out_remote(p, h).start()
        take(part.at[s, h, pl.ds(0, (groups - 1) * block), :], rs_send.at[s, h])
        take(g.at[s, h, pl.ds(0, (ZH - 1) * block), :], z_send.at[s, h])
        take(g.at[s, h, pl.ds(0, (X - 1) * wide), :], x_send.at[s, h])

    rhs_local(0).wait()
    take(bb.at[0, mine, :], b_recv.at[0])
    for h in range(chunks):
        g[0, h, here, :] = bb[0, :, pl.ds(h * LANES, LANES)].astype(BF16)
        gather_start(0, h)
    for p in range(1, panels):
        rhs_local(p).start()
        rhs_remote(p).start()
    for f in order[1:]:
        factor_local(f).start()
        factor_remote(f).start()

    for s in range(len(stages)):
        for h in range(chunks):
            relay_and_first(s, h)
        for h in range(chunks):
            finish_product(s, h)
        p, inverse = stages[s]
        if not inverse:
            rhs_local(p).wait()
            take(bb.at[p, mine, :], b_recv.at[p])
        for h in range(chunks):
            reduce_and_send(s, h)

    for p in range(panels):
        rhs_remote(p).wait_send()
        for h in range(chunks):
            out_local(p, h).wait()
            out_remote(p, h).wait_send()
            take(xo.at[p, h, mine, :], o_recv.at[p, h])
    for f in order:
        factor_remote(f).wait_send()


def body(right_side, inverse_blocks, lower_blocks):
    panels, _, rows, columns = right_side.shape
    groups, depth = inverse_blocks.shape[1], inverse_blocks.shape[3]
    factors = panels + lower_blocks.shape[0]
    half = columns // CORE
    chunks = half // LANES
    block = rows * CORE
    steps = 2 * panels - 1
    dma = pltpu.SemaphoreType.DMA
    return pl.pallas_call(
        functools.partial(solve_kernel, panels),
        out_shape=jax.ShapeDtypeStruct(right_side.shape, F32),
        in_specs=[pl.BlockSpec(memory_space=pl.ANY)] * 3,
        out_specs=pl.BlockSpec(memory_space=pl.ANY),
        scratch_shapes=[
            pltpu.VMEM((factors, groups, block, depth), BF16),
            pltpu.VMEM((panels, block, half), F32),
            pltpu.VMEM((steps, chunks, depth, LANES), BF16),
            pltpu.VMEM((steps, chunks, groups * block, LANES), BF16),
            pltpu.VMEM((steps, chunks, groups, block, LANES), BF16),
            pltpu.VMEM((panels, chunks, block, LANES), F32),
            pltpu.VMEM((chunks, groups * block, LANES), F32),
            pltpu.VMEM((panels - 2, chunks, groups * block, LANES), F32),
            dma((panels,)), dma((panels,)), dma((panels,)),
            dma((factors,)), dma((factors,)), dma((factors,)),
            dma((steps, chunks)), dma((steps, chunks)),
            dma((steps, chunks)), dma((steps, chunks, ZH - 1)),
            dma((steps, chunks)), dma((steps, chunks, X - 1)),
            dma((panels, chunks)), dma((panels, chunks)), dma((panels, chunks)),
        ],
        compiler_params=pltpu.CompilerParams(
            collective_id=0, has_side_effects=True, vmem_limit_bytes=40 * 1024 * 1024
        ),
        cost_estimate=pl.CostEstimate(
            flops=2 * factors * groups * rows * depth * columns,
            bytes_accessed=2 * factors * groups * rows * depth, transcendentals=0,
        ),
        name="solve",
    )(right_side, inverse_blocks, lower_blocks)


def solution(mesh):
    return jax.shard_map(
        body,
        mesh=mesh,
        in_specs=(
            P(None, "cols", "rows", None),
            P(None, None, "rows", "cols"),
            P(None, None, "rows", "cols"),
        ),
        out_specs=P(None, "cols", "rows", None),
        check_vma=False,
    )
```

time: 678 us -> 116 us (0.17)
  waiting for transfers between devices: 625 us -> 0 us
  Pallas kernels: 0 us -> 110 us
  matrix products: 23.2 us -> 0 us
  between operations: 13.3 us -> 0.01 us
  other arithmetic: 10.3 us -> 0 us
    all_gather x7 -> x0, waiting for transfers between devices: 397 us -> none  [the longest x4 230 us: forward_solve(): lax.all_gather(residual, 'rows', axis=1, tiled=True)]
    reduce_scatter x7 -> x0, waiting for transfers between devices: 227 us -> none  [the longest x4 130 us: forward_solve(): solved = lax.psum_scatter(products, 'cols', scatter_dimension=0, tiled=True)]
    pallas_call x0 -> x1, Pallas kernels: none -> 110 us  [body(): pl.pallas_call(functools.partial(solve_kernel, panels), out_shape=jax.Sha...]
    dot_general x10 -> x0, matrix products: 23.2 us -> none  [the longest x6 13.2 us: product(): jnp.einsum('abk,kn->abn', factor_block, rows_all, preferred_element_type=...]
    convert_element_type x6 -> x0, other arithmetic: 8.77 us -> none  [the longest x3 4.39 us: forward_solve(): residual = (right_side[current] - shares).astype(jnp.bfloat16)]
  transfers between devices with their start and end apart: 14 -> 0, of which waited for: 14 -> 0; matrix products, arithmetic and copies ran while one was open for 1% -> 0% of each run, Pallas kernels for 0% -> 0%
where the time goes in v1:
time: 116 us
  Pallas kernels  110 us (95%)
  local copies, waits for them, and re-layouts  5.13 us (4%)
    pallas_call x1, Pallas kernels, body(): pl.pallas_call(functools.partial(solve_kernel, panels), out_shape=jax.Sha...  110 us
    unnamed x7, local copies, waits for them, and re-layouts  5.13 us

profile of v1, /device:TPU:1, one launch (start us, length us, event | category | flops | bytes accessed | tf_op | source)
XLA Modules:
  0.0 115.5 jit_solution(13615962038555520163)
XLA Ops:
  0.0 0.0 copy-start
  0.0 1.9 %copy-done = bf16[6,8,32,1024]{3,2,1,0:T(8,128)(2,1)S(1)} copy-done((bf16[6,8,32,1024]{3,2,1,0:T(8,128)(2,1)S(1)}, bf16[6,8,32,1024]{3,2,1,0:T(8,128)(2,1)}, u32[]{:S(2)}) %copy-start) | copy-done | bytes 3145752
  1.9 0.0 copy-start.1
  1.9 1.6 %copy-done.1 = bf16[4,8,32,1024]{3,2,1,0:T(8,128)(2,1)S(1)} copy-done((bf16[4,8,32,1024]{3,2,1,0:T(8,128)(2,1)S(1)}, bf16[4,8,32,1024]{3,2,1,0:T(8,128)(2,1)}, u32[]{:S(2)}) %copy-start.1) | copy-done | bytes 2097176
  3.5 0.0 copy-start.2
  3.5 0.9 copy-done.2
  4.4 110.4 %solve.1 = f32[4,1,32,512]{3,2,1,0:T(8,128)S(1)} custom-call(f32[4,1,32,512]{3,2,1,0:T(8,128)S(1)} %copy-done.2, bf16[4,8,32,1024]{3,2,1,0:T(8,128)(2,1)S(1)} %copy-done.1, bf16[6,8,32,1024]{3,2,1,0:T(8,128)(2,1)S(1)} %copy-done), custom_call_target="tpu_custom_call" | custom-call | flops 2684354560 | bytes 5242880 | tf_op jit(solution)/shard_map/solve/pallas_call | solution.py:253
  114.8 0.7 copy.5
Async XLA Ops:
  0.0 1.9 %copy-start = (bf16[6,8,32,1024]{3,2,1,0:T(8,128)(2,1)S(1)}, bf16[6,8,32,1024]{3,2,1,0:T(8,128)(2,1)}, u32[]{:S(2)}) copy-start(bf16[6,8,32,1024]{3,2,1,0:T(8,128)(2,1)} %low.1) | copy-start | bytes 9437188
  1.9 1.6 %copy-start.1 = (bf16[4,8,32,1024]{3,2,1,0:T(8,128)(2,1)S(1)}, bf16[4,8,32,1024]{3,2,1,0:T(8,128)(2,1)}, u32[]{:S(2)}) copy-start(bf16[4,8,32,1024]{3,2,1,0:T(8,128)(2,1)} %inv.1) | copy-start | bytes 6291460
  3.5 0.9 copy-start.2
